TPU v7x, 256 devices: a whole 4x4x8 slice. The times are simulated.
256 devices in a mesh: replica: 32 (over x_lo, z, core), tensor: 8 (over y, x_hi).
Axes of the slice: x: 4 (x_hi: 2, x_lo: 2; x = x_hi * 2 + x_lo), y: 4, z: 8, core: 2. Of those that a mesh axis runs over, the one named last changes fastest.
Arguments:
- inputs: bfloat16 [2, 16384, 2048], P(None, 'replica', 'tensor'), may hold values from -6 to 6
- out_grads: bfloat16 [2, 16384, 2048], P(None, 'replica', 'tensor'), may hold values from -6 to 6
- gate_weight: bfloat16 [32, 2048, 2816], P('replica', None, 'tensor'), may hold values from -0.125 to 0.125
- up_weight: bfloat16 [32, 2048, 2816], P('replica', None, 'tensor'), may hold values from -0.125 to 0.125
- down_weight: bfloat16 [32, 2816, 2048], P('replica', 'tensor'), may hold values from -0.109375 to 0.109375
- rates: float32 [32], P('replica'), may hold values from 16 to 64
- partner_bits: int32 [4], replicated, may hold values from 0 to 3, each once
Outputs:
- new_gate: bfloat16 [32, 2048, 2816], P('replica', None, 'tensor')
- new_up: bfloat16 [32, 2048, 2816], P('replica', None, 'tensor')
- new_down: bfloat16 [32, 2816, 2048], P('replica', 'tensor')
- activations: bfloat16 [2, 16384, 2048], P(None, 'replica', 'tensor')
Inputs may be any that keep to these rules, and one draw needn't show every extreme that they name: partner_bits holds each of the bit numbers 0, 1, 2, 3 exactly once; step s uses entry s.
All inputs are finite; a program needn't handle non-finite values.
Results may differ from a plain program's by a relative error of at most 0.024.
Values may be sent and summed in bfloat16 or wider, within the bound.
No kernel may reach another device: no remote copies, remote signals or barrier semaphores. Data moves between devices by JAX's collectives and lax.ppermute only.
A program may use at most 128 MiB of HBM per device.

v0:
```python
from functools import partial
import jax
import jax.numpy as jnp
from jax import lax
from jax.sharding import PartitionSpec as P


def shortened(value):

    def short(part):
        return part.astype(jnp.bfloat16) if part.dtype == jnp.float32 else part

    return jax.tree.map(short, value)


def partner(value, axis, distance):
    mask = 2**distance
    pairs = [(source, source ^ mask) for source in range(lax.axis_size(axis))]
    return lax.ppermute(value, axis, pairs)


def local_pass(weights, inputs, grads_out):
    gate_w, up_w, down_w = weights
    gate = jnp.dot(inputs, gate_w, preferred_element_type=jnp.float32)
    up = jnp.dot(inputs, up_w, preferred_element_type=jnp.float32)
    sigma = jax.nn.sigmoid(gate)
    active = gate * sigma
    hidden = (active * up).astype(jnp.bfloat16)
    mixed = jnp.dot(hidden, down_w, preferred_element_type=jnp.float32)
    back = lax.dot_general(
        grads_out, down_w, (((1,), (1,)), ((), ())), preferred_element_type=jnp.float32
    )
    d_gate = (back * up * sigma * (1.0 + gate * (1.0 - sigma))).astype(jnp.bfloat16)
    d_up = (back * active).astype(jnp.bfloat16)
    grad_down = lax.dot_general(
        hidden, grads_out, (((0,), (0,)), ((), ())), preferred_element_type=jnp.float32
    )
    grad_gate = lax.dot_general(
        inputs, d_gate, (((0,), (0,)), ((), ())), preferred_element_type=jnp.float32
    )
    grad_up = lax.dot_general(
        inputs, d_up, (((0,), (0,)), ((), ())), preferred_element_type=jnp.float32
    )
    return (mixed, (grad_gate, grad_up, grad_down))


def squares_of(grads):
    return sum((jnp.sum(g * g) for g in grads))


def apply_update(weights, grads, squares, rate):
    scale = rate / jnp.sqrt(squares + 1e-06)
    return tuple(
        ((w.astype(jnp.float32) - scale * g).astype(jnp.bfloat16) for w, g in zip(weights, grads))
    )


def average(first, second):
    return tuple(
        (
            ((a.astype(jnp.float32) + b.astype(jnp.float32)) * 0.5).astype(jnp.bfloat16)
            for a, b in zip(first, second)
        )
    )


def total_norms(values):
    return lax.psum((values[0],), "tensor")


def mixing_bit(bit_number, values):
    return jax.tree.map(
        lambda piece: jax.tree.map(
            lambda part, own: part.astype(own.dtype),
            partner(shortened(piece), "replica", bit_number),
            piece,
        ),
        values,
    )


def partner_values(values, bit, handler):
    branches = [partial(handler, number) for number in range(4)]
    return lax.switch(bit, branches, values)


def local(inputs, out_grads, gate_weight, up_weight, down_weight, rates, partner_bits):
    weights = (gate_weight[0], up_weight[0], down_weight[0])
    results = []
    for step in range(inputs.shape[0]):
        whole_x, whole_dy = (
            lax.all_gather(inputs[step], "tensor", axis=1, tiled=True),
            lax.all_gather(out_grads[step], "tensor", axis=1, tiled=True),
        )
        bit = partner_bits[step]
        mixed, grads = local_pass(weights, whole_x, whole_dy)
        squares = total_norms((squares_of(grads),))[0]
        fresh = apply_update(weights, grads, squares, rates[0])
        other = partner_values(fresh, bit, mixing_bit)
        weights = average(fresh, other)
        summed = lax.psum_scatter(
            mixed.astype(jnp.bfloat16), "tensor", scatter_dimension=1, tiled=True
        )
        results.append(summed)
    return (weights[0][None], weights[1][None], weights[2][None], jnp.stack(results))


def solution(mesh):
    return jax.shard_map(
        local,
        mesh=mesh,
        in_specs=(
            P(None, "replica", "tensor"),
            P(None, "replica", "tensor"),
            P("replica", None, "tensor"),
            P("replica", None, "tensor"),
            P("replica", "tensor", None),
            P("replica"),
            P(),
        ),
        out_specs=(
            P("replica", None, "tensor"),
            P("replica", None, "tensor"),
            P("replica", "tensor", None),
            P(None, "replica", "tensor"),
        ),
        check_vma=False,
    )
```

profile of v0, /device:TPU:32, one launch (start us, length us, event | category | flops | bytes accessed | tf_op | source)
XLA Modules:
  0.0 427.8 jit_solution(12777738690879736687)
XLA Ops:
  13.8 59.1 %all-gather.11.cloned.1.call-done = bf16[1,512,2048]{2,1,0:T(8,128)(2,1)} async-done(((bf16[1,512,256]{2,1,0:T(8,128)(2,1)}), bf16[1,512,2048]{2,1,0:T(8,128)(2,1)}) %all-gather.11.cloned.1.call-update) | async-done | bytes 2097168 | tf_op jit(solution)/shard_map/all_gather | solution.py:92
  80.2 52.8 %all-gather.9.cloned.1.call-done = bf16[1,512,2048]{2,1,0:T(8,128)(2,1)} async-done(((bf16[1,512,256]{2,1,0:T(8,128)(2,1)}), bf16[1,512,2048]{2,1,0:T(8,128)(2,1)}) %all-gather.9.cloned.1.call-update) | async-done | bytes 2097168 | tf_op jit(solution)/shard_map/all_gather | solution.py:93
  135.7 3.2 multiply_reduce_fusion.4
  138.9 3.3 multiply_reduce_fusion.5
  143.5 3.2 multiply_reduce_fusion.3
  147.9 20.4 %psum.14 = f32[]{:T(128)} all-reduce(f32[]{:T(128)S(6)} %add.59), channel_id=1, replica_groups=mesh['replica'=32,'tensor'=8] {'tensor'}, use_global_device_ids=true, to_apply=%region_3.0 | all-reduce | flops 1 | bytes 8 | tf_op jit(solution)/shard_map/psum | solution.py:68
  175.0 90.9 %conditional.8 = (bf16[2048,352]{0,1:T(8,128)(2,1)}, bf16[352,2048]{1,0:T(8,128)(2,1)}, bf16[2048,352]{0,1:T(8,128)(2,1)}) conditional(s32[]{:T(128)} %bitcast.7, (bf16[2048,352]{0,1:T(8,128)(2,1)S(1)}, bf16[2048,352]{0,1:T(8,128)(2,1)S(1)}, bf16[352,2048]{1,0:T(8,128)(2,1)S(1)}) %tuple.108, ...), branch_computations={%region_4.0_spmd, %region_5.0_spmd, %region_6.0_spmd, %region_7.0_... | conditional | bytes 17301648
  177.6 32.1 %collective-permute-done.3 = bf16[2048,352]{0,1:T(8,128)(2,1)} collective-permute-done((bf16[2048,352]{0,1:T(8,128)(2,1)S(1)}, bf16[2048,352]{0,1:T(8,128)(2,1)}, u32[]{:S(2)}, u32[]{:S(2)}) %collective-permute-start.3) | collective-permute-done | bytes 1441824 | tf_op jit(solution)/shard_map/cond/branch_1_fun/ppermute | solution.py:19
  209.7 30.9 %collective-permute-done.4 = bf16[2048,352]{0,1:T(8,128)(2,1)} collective-permute-done((bf16[2048,352]{0,1:T(8,128)(2,1)S(1)}, bf16[2048,352]{0,1:T(8,128)(2,1)}, u32[]{:S(2)}, u32[]{:S(2)}) %collective-permute-start.4) | collective-permute-done | bytes 1441824 | tf_op jit(solution)/shard_map/cond/branch_1_fun/ppermute | solution.py:19
  240.6 25.3 %collective-permute-done.5 = bf16[352,2048]{1,0:T(8,128)(2,1)} collective-permute-done((bf16[352,2048]{1,0:T(8,128)(2,1)S(1)}, bf16[352,2048]{1,0:T(8,128)(2,1)}, u32[]{:S(2)}, u32[]{:S(2)}) %collective-permute-start.5) | collective-permute-done | bytes 1441824 | tf_op jit(solution)/shard_map/cond/branch_1_fun/ppermute | solution.py:19
  265.9 3.1 fusion.53
  269.1 3.5 multiply_convert_fusion
  272.6 4.0 convolution_convert_fusion
  276.6 3.2 fusion.47
  279.9 3.1 multiply_reduce_fusion.1
  283.0 3.3 multiply_reduce_fusion.2
  287.5 3.2 multiply_reduce_fusion
  292.0 22.9 %psum.15 = f32[]{:T(128)} all-reduce(f32[]{:T(128)S(6)} %add.67), channel_id=1, replica_groups=mesh['replica'=32,'tensor'=8] {'tensor'}, use_global_device_ids=true, to_apply=%region_11.0 | all-reduce | flops 1 | bytes 8 | tf_op jit(solution)/shard_map/psum | solution.py:68
  319.0 4.4 %fusion.12 = (bf16[2048,352]{0,1:T(8,128)(2,1)S(1)}, bf16[2048,352]{0,1:T(8,128)(2,1)S(1)}) fusion(f32[352,2048]{1,0:T(8,128)S(1)} %copy-done.10, f32[]{:T(128)S(6)} %div.15, bf16[2048,352]{0,1:T(8,128)(2,1)} %get-tuple-element.159, bf16[2048,352]{0,1:T(8,128)(2,1)S(1)} %copy-done.5, f32[352,2048]{1,0:T(8,128)} %get-tuple-element.181, ...), kind=kLoop, calls=%fused_computation.21 | loop fusion | flops 12976128 | bytes 14417924 | tf_op jit(solution)/shard_map/convert_element_type | solution.py:54
  323.5 7.6 %conditional.9 = (bf16[2048,352]{0,1:T(8,128)(2,1)}, bf16[2048,352]{0,1:T(8,128)(2,1)}, bf16[352,2048]{1,0:T(8,128)(2,1)}) conditional(s32[]{:T(128)} %bitcast.15, (bf16[2048,352]{0,1:T(8,128)(2,1)S(1)}, bf16[2048,352]{0,1:T(8,128)(2,1)S(1)}, bf16[352,2048]{1,0:T(8,128)(2,1)S(1)}) %tuple.109, ...), branch_computations={%region_12.0_spmd, %region_13.0_spmd, %region_14.0_spmd, %region_1... | conditional | bytes 17301648
  331.0 3.1 fusion.40
  334.1 3.0 fusion.42
  337.1 3.0 fusion.41
  340.1 79.1 %reduce-scatter.5.cloned.1.call-done = bf16[512,256]{1,0:T(8,128)(2,1)} async-done(((bf16[512,2048]{1,0:T(8,128)(2,1)}), bf16[512,256]{1,0:T(8,128)(2,1)}) %reduce-scatter.5.cloned.1.call-update) | async-done | bytes 262160 | tf_op jit(solution)/shard_map/reduce_scatter | solution.py:101
  (90 shorter events, 37.4 us)
Async XLA Ops:
  7.2 6.0 %copy-start.16 = (s32[4]{0:T(128)S(1)}, s32[4]{0:T(128)}, u32[]{:S(2)}) copy-start(s32[4]{0:T(128)} %param.21) | copy-start | bytes 52
  7.2 65.7 %copy-start.14 = (bf16[1,2048,352]{1,2,0:T(8,128)(2,1)S(1)}, bf16[1,2048,352]{1,2,0:T(8,128)(2,1)}, u32[]{:S(2)}) copy-start(bf16[1,2048,352]{1,2,0:T(8,128)(2,1)} %param.17) | copy-start | bytes 4325380
  7.2 65.6 %all-gather.11.cloned.1.call-start = ((), (), s32[]{:S(2)}) async-start(), calls=%async_computation.5 | async-start | bytes 2359296 | tf_op jit(solution)/shard_map/all_gather | solution.py:92
  9.2 123.7 %all-gather.9.cloned.1.call-start = ((), (), s32[]{:S(2)}) async-start(), calls=%async_computation.4 | async-start | bytes 2359296 | tf_op jit(solution)/shard_map/all_gather | solution.py:93
  11.2 254.7 %all-gather.15.cloned.1.call-start = ((), (), s32[]{:S(2)}) async-start(), calls=%async_computation.7 | async-start | bytes 2359296 | tf_op jit(solution)/shard_map/all_gather | solution.py:92
  11.9 264.7 %all-gather.13.cloned.1.call-start = ((), (), s32[]{:S(2)}) async-start(), calls=%async_computation.6 | async-start | bytes 2359296 | tf_op jit(solution)/shard_map/all_gather | solution.py:93
  12.5 327.6 %reduce-scatter.3.cloned.1.call-start = ((), (), s32[]{:S(2)}) async-start(), calls=%async_computation.2 | async-start | bytes 2359296 | tf_op jit(solution)/shard_map/reduce_scatter | solution.py:101
  13.8 61.8 %copy-start.12 = (bf16[1,2048,352]{1,2,0:T(8,128)(2,1)S(1)}, bf16[1,2048,352]{1,2,0:T(8,128)(2,1)}, u32[]{:S(2)}) copy-start(bf16[1,2048,352]{1,2,0:T(8,128)(2,1)} %param.18) | copy-start | bytes 4325380
  80.2 55.5 %copy-start.22 = (f32[512,352]{0,1:T(8,128)S(1)}, f32[512,352]{0,1:T(8,128)}, u32[]{:S(2)}) copy-start(f32[512,352]{0,1:T(8,128)} %copy-done.21) | copy-start | bytes 2162692
  80.2 338.9 %reduce-scatter.5.cloned.1.call-start = ((), (), s32[]{:S(2)}) async-start(), calls=%async_computation.3 | async-start | bytes 2359296 | tf_op jit(solution)/shard_map/reduce_scatter | solution.py:101
  171.1 3.9 copy-start.2
  172.2 96.9 %copy-start.4 = (bf16[2048,352]{0,1:T(8,128)(2,1)}, bf16[2048,352]{0,1:T(8,128)(2,1)S(1)}, u32[]{:S(2)}) copy-start(bf16[2048,352]{0,1:T(8,128)(2,1)S(1)} %fusion.14) | copy-start | bytes 4325380
  175.0 94.0 %copy-start.6 = (bf16[2048,352]{0,1:T(8,128)(2,1)}, bf16[2048,352]{0,1:T(8,128)(2,1)S(1)}, u32[]{:S(2)}) copy-start(bf16[2048,352]{0,1:T(8,128)(2,1)S(1)} %fusion.15) | copy-start | bytes 4325380
  175.0 34.6 %collective-permute-start.3 = (bf16[2048,352]{0,1:T(8,128)(2,1)S(1)}, bf16[2048,352]{0,1:T(8,128)(2,1)}, u32[]{:S(2)}, u32[]{:S(2)}) collective-permute-start(bf16[2048,352]{0,1:T(8,128)(2,1)S(1)} %get-tuple-element.87), channel_id=1, source_target_pairs={{0,16},{8,24},{16,0},{24,8},{32,48},{40,56},{48,32},{56,40},{64,80... | collective-permute-start | bytes 4325384 | tf_op jit(solution)/shard_map/cond/branch_1_fun/ppermute | solution.py:19
  175.6 65.0 %collective-permute-start.4 = (bf16[2048,352]{0,1:T(8,128)(2,1)S(1)}, bf16[2048,352]{0,1:T(8,128)(2,1)}, u32[]{:S(2)}, u32[]{:S(2)}) collective-permute-start(bf16[2048,352]{0,1:T(8,128)(2,1)S(1)} %get-tuple-element.88), channel_id=1, source_target_pairs={{0,16},{8,24},{16,0},{24,8},{32,48},{40,56},{48,32},{56,40},{64,80... | collective-permute-start | bytes 4325384 | tf_op jit(solution)/shard_map/cond/branch_1_fun/ppermute | solution.py:19
  177.2 88.7 %collective-permute-start.5 = (bf16[352,2048]{1,0:T(8,128)(2,1)S(1)}, bf16[352,2048]{1,0:T(8,128)(2,1)}, u32[]{:S(2)}, u32[]{:S(2)}) collective-permute-start(bf16[352,2048]{1,0:T(8,128)(2,1)S(1)} %get-tuple-element.89), channel_id=1, source_target_pairs={{0,16},{8,24},{16,0},{24,8},{32,48},{40,56},{48,32},{56,40},{64,80... | collective-permute-start | bytes 4325384 | tf_op jit(solution)/shard_map/cond/branch_1_fun/ppermute | solution.py:19
  269.0 3.5 copy-start.23
  269.1 3.5 copy-start.3
  276.6 3.2 copy-start.24
  315.5 3.5 copy-start.10
  318.2 5.3 %copy-start = (bf16[352,2048]{1,0:T(8,128)(2,1)}, bf16[352,2048]{1,0:T(8,128)(2,1)S(1)}, u32[]{:S(2)}) copy-start(bf16[352,2048]{1,0:T(8,128)(2,1)S(1)} %subtract_convert_fusion) | copy-start | bytes 4325380
  323.5 3.4 collective-permute-start.12
  323.6 5.4 %collective-permute-start.13 = (bf16[2048,352]{0,1:T(8,128)(2,1)S(1)}, bf16[2048,352]{0,1:T(8,128)(2,1)}, u32[]{:S(2)}, u32[]{:S(2)}) collective-permute-start(bf16[2048,352]{0,1:T(8,128)(2,1)S(1)} %get-tuple-element.97), channel_id=1, source_target_pairs={{0,8},{8,0},{16,24},{24,16},{32,40},{40,32},{48,56},{56,48},{64,72... | collective-permute-start | bytes 4325384 | tf_op jit(solution)/shard_map/cond/branch_0_fun/ppermute | solution.py:19
  324.1 7.0 %collective-permute-start.14 = (bf16[352,2048]{1,0:T(8,128)(2,1)S(1)}, bf16[352,2048]{1,0:T(8,128)(2,1)}, u32[]{:S(2)}, u32[]{:S(2)}) collective-permute-start(bf16[352,2048]{1,0:T(8,128)(2,1)S(1)} %get-tuple-element.98), channel_id=1, source_target_pairs={{0,8},{8,0},{16,24},{24,16},{32,40},{40,32},{48,56},{56,48},{64,72... | collective-permute-start | bytes 4325384 | tf_op jit(solution)/shard_map/cond/branch_0_fun/ppermute | solution.py:19
  (15 other events, 40.6 us)
Sparse Core Ops, SparseCore 0:
  11.0 61.7 all-gather.10
  75.9 57.0 all-gather.8
  135.5 57.1 all-gather.14
  195.0 57.0 all-gather.12
  255.9 79.1 reduce-scatter.2
  339.0 80.0 reduce-scatter.4
where the time goes:
time: 428 us
  waiting for transfers between devices  287 us (67%)
  blocking collectives  43.2 us (10%)
  matrix products  43 us (10%)
  between operations  21.5 us (5%)
  other arithmetic  20.9 us (5%)
  local copies, waits for them, and re-layouts  8.34 us (2%)
    ppermute x6, waiting for transfers between devices, partner(): return lax.ppermute(value, axis, pairs)  95.1 us
    reduce_scatter x2, waiting for transfers between devices, local(): lax.psum_scatter(mixed.astype(jnp.bfloat16), 'tensor', scatter_dimension=...  79.1 us
    all_gather x2, waiting for transfers between devices, local(): lax.all_gather(inputs[step], 'tensor', axis=1, tiled=True)  59.1 us
    all_gather x2, waiting for transfers between devices, local(): lax.all_gather(out_grads[step], 'tensor', axis=1, tiled=True)  52.8 us
    psum x2, blocking collectives, total_norms(): return lax.psum((values[0],), 'tensor')  43.2 us
    convert_element_type x5, other arithmetic, apply_update(): (w.astype(jnp.float32) - scale * g).astype(jnp.bfloat16)  10 us
  transfers between devices with their start and end apart: 12, of which 9 were waited for; matrix products, arithmetic and copies ran while one was open for 15% of the time, Pallas kernels for 0%

commit v1 on v0

--- a/solution.py
+++ b/solution.py
@@ -3,6 +3,7 @@
 import jax.numpy as jnp
 from jax import lax
 from jax.sharding import PartitionSpec as P
+from jax.lax import all_to_all, axis_size
 
 
 def shortened(value):
@@ -88,8 +89,17 @@
     weights = (gate_weight[0], up_weight[0], down_weight[0])
     results = []
     for step in range(inputs.shape[0]):
+        review_the_local_data = lambda point, axis_name, on_dim: jnp.concatenate(
+            all_to_all(
+                jnp.stack([point for _ in range(axis_size(axis_name))], axis=0),
+                axis_name=axis_name,
+                split_axis=0,
+                concat_axis=0,
+            ),
+            axis=on_dim,
+        )
         whole_x, whole_dy = (
-            lax.all_gather(inputs[step], "tensor", axis=1, tiled=True),
+            review_the_local_data(inputs[step], "tensor", 1),
             lax.all_gather(out_grads[step], "tensor", axis=1, tiled=True),
         )
         bit = partner_bits[step]

time: 428 us -> 335 us (0.78)
  waiting for transfers between devices: 287 us -> 180 us
  starting transfers between devices: 3.52 us -> 14.6 us
    reduce_scatter x2, waiting for transfers between devices: 79.1 us -> 17.5 us  [local(): lax.psum_scatter(mixed.astype(jnp.bfloat16), 'tensor', scatter_dimension=...]
    all_gather x2 -> x0, waiting for transfers between devices: 59.1 us -> none  [local(): lax.all_gather(inputs[step], 'tensor', axis=1, tiled=True)]
    all_to_all x0 -> x2, waiting for transfers between devices: none -> 29.9 us  [local(): all_to_all(jnp.stack([point for _ in range(axis_size(axis_name))], axis=0...]
    all_gather x2, waiting for transfers between devices: 52.8 us -> 35.1 us  [local(): lax.all_gather(out_grads[step], 'tensor', axis=1, tiled=True)]
    all_to_all x0 -> x2, starting transfers between devices: none -> 11.6 us  [local(): all_to_all(jnp.stack([point for _ in range(axis_size(axis_name))], axis=0...]
  transfers between devices with their start and end apart: 12 -> 12, of which waited for: 9 -> 9; matrix products, arithmetic and copies ran while one was open for 15% -> 20% of each run, Pallas kernels for 0% -> 0%
where the time goes in v1:
time: 335 us; the launch traced here: 334 us
  waiting for transfers between devices  180 us (54%)
  matrix products  43 us (13%)
  blocking collectives  42.7 us (13%)
  between operations  21.1 us (6%)
  other arithmetic  20.7 us (6%)
  starting transfers between devices  14.6 us (4%)
  local copies, waits for them, and re-layouts  11.9 us (4%)
    ppermute x6, waiting for transfers between devices, partner(): return lax.ppermute(value, axis, pairs)  96.6 us
    psum x2, blocking collectives, total_norms(): return lax.psum((values[0],), 'tensor')  42.7 us
    all_gather x2, waiting for transfers between devices, local(): lax.all_gather(out_grads[step], 'tensor', axis=1, tiled=True)  35.1 us
    all_to_all x2, waiting for transfers between devices, local(): all_to_all(jnp.stack([point for _ in range(axis_size(axis_name))], axis=0...  29.9 us
    reduce_scatter x2, waiting for transfers between devices, local(): lax.psum_scatter(mixed.astype(jnp.bfloat16), 'tensor', scatter_dimension=...  17.5 us
    all_to_all x2, starting transfers between devices, local(): all_to_all(jnp.stack([point for _ in range(axis_size(axis_name))], axis=0...  11.6 us
    convert_element_type x5, other arithmetic, apply_update(): (w.astype(jnp.float32) - scale * g).astype(jnp.bfloat16)  9.86 us
    dot_general x2, matrix products, local_pass(): lax.dot_general(inputs, d_gate, (((0,), (0,)), ((), ())), preferred_eleme...  8.11 us
  transfers between devices with their start and end apart: 12, of which 9 were waited for; matrix products, arithmetic and copies ran while one was open for 20% of the time, Pallas kernels for 0%

profile of v1, /device:TPU:32, one launch (start us, length us, event | category | flops | bytes accessed | tf_op | source)
XLA Modules:
  0.0 334.1 jit_solution(11968677122626932629)
XLA Ops:
  12.6 7.1 %all-to-all-start = ((bf16[8,512,256]{1,2,0:T(8,128)(2,1)}), bf16[8,512,256]{1,2,0:T(8,128)(2,1)S(1)}, u32[]{:S(2)}, u32[]{:S(2)}) async-start(bf16[8,512,256]{1,2,0:T(8,128)(2,1)} %stack.15), calls=%async_computation | async-start | bytes 4194304 | tf_op jit(solution)/shard_map/all_to_all | solution.py:93
  21.1 29.9 %all-to-all-done = bf16[8,512,256]{1,2,0:T(8,128)(2,1)S(1)} async-done(((bf16[8,512,256]{1,2,0:T(8,128)(2,1)}), bf16[8,512,256]{1,2,0:T(8,128)(2,1)S(1)}, u32[]{:S(2)}, u32[]{:S(2)}) %all-to-all-start) | async-done | bytes 2097184 | tf_op jit(solution)/shard_map/all_to_all | solution.py:93
  52.5 4.5 %all-to-all-start.1 = ((bf16[8,512,256]{1,2,0:T(8,128)(2,1)}), bf16[8,512,256]{1,2,0:T(8,128)(2,1)}, u32[]{:S(2)}, u32[]{:S(2)}) async-start(bf16[8,512,256]{1,2,0:T(8,128)(2,1)} %stack.16), calls=%async_computation.1 | async-start | bytes 4194304 | tf_op jit(solution)/shard_map/all_to_all | solution.py:93
  63.7 35.1 %all-gather.5.cloned.1.call-done = bf16[1,512,2048]{2,1,0:T(8,128)(2,1)} async-done(((bf16[1,512,256]{2,1,0:T(8,128)(2,1)}), bf16[1,512,2048]{2,1,0:T(8,128)(2,1)}) %all-gather.5.cloned.1.call-update) | async-done | bytes 2097168 | tf_op jit(solution)/shard_map/all_gather | solution.py:103
  101.4 3.1 multiply_reduce_fusion.4
  104.6 3.2 multiply_reduce_fusion.5
  112.0 20.0 %psum.14 = f32[]{:T(128)} all-reduce(f32[]{:T(128)S(6)} %add.59), channel_id=1, replica_groups=mesh['replica'=32,'tensor'=8] {'tensor'}, use_global_device_ids=true, to_apply=%region_3.0 | all-reduce | flops 1 | bytes 8 | tf_op jit(solution)/shard_map/psum | solution.py:69
  138.6 92.0 %conditional.8 = (bf16[2048,352]{0,1:T(8,128)(2,1)}, bf16[352,2048]{1,0:T(8,128)(2,1)}, bf16[2048,352]{0,1:T(8,128)(2,1)}) conditional(s32[]{:T(128)} %bitcast.10, (bf16[2048,352]{0,1:T(8,128)(2,1)S(1)}, bf16[2048,352]{0,1:T(8,128)(2,1)S(1)}, bf16[352,2048]{1,0:T(8,128)(2,1)S(1)}) %tuple.108, ...), branch_computations={%region_4.0_spmd, %region_5.0_spmd, %region_6.0_spmd, %region_7.0_... | conditional | bytes 17301648
  140.9 32.4 %collective-permute-done.3 = bf16[2048,352]{0,1:T(8,128)(2,1)} collective-permute-done((bf16[2048,352]{0,1:T(8,128)(2,1)S(1)}, bf16[2048,352]{0,1:T(8,128)(2,1)}, u32[]{:S(2)}, u32[]{:S(2)}) %collective-permute-start.3) | collective-permute-done | bytes 1441824 | tf_op jit(solution)/shard_map/cond/branch_1_fun/ppermute | solution.py:20
  173.3 30.9 %collective-permute-done.4 = bf16[2048,352]{0,1:T(8,128)(2,1)} collective-permute-done((bf16[2048,352]{0,1:T(8,128)(2,1)S(1)}, bf16[2048,352]{0,1:T(8,128)(2,1)}, u32[]{:S(2)}, u32[]{:S(2)}) %collective-permute-start.4) | collective-permute-done | bytes 1441824 | tf_op jit(solution)/shard_map/cond/branch_1_fun/ppermute | solution.py:20
  204.2 26.4 %collective-permute-done.5 = bf16[352,2048]{1,0:T(8,128)(2,1)} collective-permute-done((bf16[352,2048]{1,0:T(8,128)(2,1)S(1)}, bf16[352,2048]{1,0:T(8,128)(2,1)}, u32[]{:S(2)}, u32[]{:S(2)}) %collective-permute-start.5) | collective-permute-done | bytes 1441824 | tf_op jit(solution)/shard_map/cond/branch_1_fun/ppermute | solution.py:20
  233.6 4.1 %multiply_convert_fusion = (bf16[512,352]{0,1:T(8,128)(2,1)S(1)}, f32[512,352]{0,1:T(8,128)}) fusion(f32[512,352]{0,1:T(8,128)S(1)} %convolution_bitcast_fusion, bf16[512,2048]{0,1:T(8,128)(2,1)} %bitcast.16, bf16[2048,352]{0,1:T(8,128)(2,1)} %get-tuple-element.183, bf16[2048,352]{0,1:T(8,128)(2,1)S(1)} %fusion.14), kind=kOutput, calls=%fused_computation.56 | convolution fusion | flops 742883328 | bytes 6782976 | tf_op jit(solution)/shard_map/dot_general | solution.py:26
  237.7 4.0 %convolution_convert_fusion = bf16[512,2048]{1,0:T(8,128)(2,1)} fusion(bf16[512,352]{0,1:T(8,128)(2,1)S(1)} %get-tuple-element.208, bf16[352,2048]{1,0:T(8,128)(2,1)} %get-tuple-element.182, bf16[352,2048]{1,0:T(8,128)(2,1)S(1)} %copy-done.3), kind=kOutput, calls=%fused_computation | convolution fusion | flops 742850560 | bytes 5341184 | tf_op jit(solution)/shard_map/dot_general | solution.py:30
  241.8 3.0 fusion.33
  244.9 4.8 %multiply_reduce_fusion.1 = (f32[]{:T(128)}, f32[352,2048]{1,0:T(8,128)}) fusion(bf16[512,2048]{0,1:T(8,128)(2,1)} %bitcast.16, f32[512,352]{0,1:T(8,128)S(1)} %fusion.33, f32[512,352]{0,1:T(8,128)S(1)} %copy-done.21), kind=kOutput, calls=%fused_computation.30 | convolution fusion | flops 740720640 | bytes 6422532 | tf_op jit(solution)/shard_map/dot_general | solution.py:42
  249.7 4.9 %multiply_reduce_fusion.2 = (f32[]{:T(128)}, f32[352,2048]{1,0:T(8,128)}) fusion(bf16[512,2048]{0,1:T(8,128)(2,1)} %bitcast.16, f32[512,352]{0,1:T(8,128)S(1)} %copy-done.21, f32[512,352]{0,1:T(8,128)S(1)} %fusion.33, f32[512,352]{0,1:T(8,128)S(1)} %copy-done.25), kind=kOutput, calls=%fused_computation.31 | convolution fusion | flops 741441536 | bytes 7143428 | tf_op jit(solution)/shard_map/dot_general | solution.py:39
  255.8 3.3 multiply_reduce_fusion
  260.3 22.8 %psum.15 = f32[]{:T(128)} all-reduce(f32[]{:T(128)S(6)} %add.67), channel_id=1, replica_groups=mesh['replica'=32,'tensor'=8] {'tensor'}, use_global_device_ids=true, to_apply=%region_11.0 | all-reduce | flops 1 | bytes 8 | tf_op jit(solution)/shard_map/psum | solution.py:69
  287.3 4.2 %fusion.12 = (bf16[2048,352]{0,1:T(8,128)(2,1)S(1)}, bf16[2048,352]{0,1:T(8,128)(2,1)S(1)}) fusion(f32[352,2048]{1,0:T(8,128)S(1)} %copy-done.10, f32[]{:T(128)S(6)} %div.15, bf16[2048,352]{0,1:T(8,128)(2,1)} %get-tuple-element.183, bf16[2048,352]{0,1:T(8,128)(2,1)S(1)} %copy-done.5, f32[352,2048]{1,0:T(8,128)} %get-tuple-element.205, ...), kind=kLoop, calls=%fused_computation.21 | loop fusion | flops 12976128 | bytes 14417924 | tf_op jit(solution)/shard_map/convert_element_type | solution.py:55
  291.6 7.6 %conditional.9 = (bf16[2048,352]{0,1:T(8,128)(2,1)}, bf16[2048,352]{0,1:T(8,128)(2,1)}, bf16[352,2048]{1,0:T(8,128)(2,1)}) conditional(s32[]{:T(128)} %bitcast.21, (bf16[2048,352]{0,1:T(8,128)(2,1)S(1)}, bf16[2048,352]{0,1:T(8,128)(2,1)S(1)}, bf16[352,2048]{1,0:T(8,128)(2,1)S(1)}) %tuple.109, ...), branch_computations={%region_12.0_spmd, %region_13.0_spmd, %region_14.0_spmd, %region_1... | conditional | bytes 17301648
  299.2 3.1 fusion.24
  302.2 3.0 fusion.26
  305.2 3.0 fusion.25
  308.2 17.5 %reduce-scatter.5.cloned.1.call-done = bf16[512,256]{1,0:T(8,128)(2,1)} async-done(((bf16[512,2048]{1,0:T(8,128)(2,1)}), bf16[512,256]{1,0:T(8,128)(2,1)}) %reduce-scatter.5.cloned.1.call-update) | async-done | bytes 262160 | tf_op jit(solution)/shard_map/reduce_scatter | solution.py:111
  (90 shorter events, 42.6 us)
Async XLA Ops:
  7.2 91.6 %all-gather.5.cloned.1.call-start = ((), (), s32[]{:S(2)}) async-start(), calls=%async_computation.6 | async-start | bytes 2359296 | tf_op jit(solution)/shard_map/all_gather | solution.py:103
  9.1 232.7 %all-gather.7.cloned.1.call-start = ((), (), s32[]{:S(2)}) async-start(), calls=%async_computation.7 | async-start | bytes 2359296 | tf_op jit(solution)/shard_map/all_gather | solution.py:103
  12.6 7.9 %copy-start.19 = (s32[4]{0:T(128)S(1)}, s32[4]{0:T(128)}, u32[]{:S(2)}) copy-start(s32[4]{0:T(128)} %param.21) | copy-start | bytes 52
  12.6 38.4 %all-to-all-start = ((bf16[8,512,256]{1,2,0:T(8,128)(2,1)}), bf16[8,512,256]{1,2,0:T(8,128)(2,1)S(1)}, u32[]{:S(2)}, u32[]{:S(2)}) async-start(bf16[8,512,256]{1,2,0:T(8,128)(2,1)} %stack.15), calls=%async_computation | async-start | bytes 4194304 | tf_op jit(solution)/shard_map/all_to_all | solution.py:93
  52.5 4.6 %copy-start.15 = (bf16[1,2048,352]{1,2,0:T(8,128)(2,1)S(1)}, bf16[1,2048,352]{1,2,0:T(8,128)(2,1)}, u32[]{:S(2)}) copy-start(bf16[1,2048,352]{1,2,0:T(8,128)(2,1)} %param.17) | copy-start | bytes 4325380
  52.5 178.1 %all-to-all-start.1 = ((bf16[8,512,256]{1,2,0:T(8,128)(2,1)}), bf16[8,512,256]{1,2,0:T(8,128)(2,1)}, u32[]{:S(2)}, u32[]{:S(2)}) async-start(bf16[8,512,256]{1,2,0:T(8,128)(2,1)} %stack.16), calls=%async_computation.1 | async-start | bytes 4194304 | tf_op jit(solution)/shard_map/all_to_all | solution.py:93
  57.0 251.1 %reduce-scatter.3.cloned.1.call-start = ((), (), s32[]{:S(2)}) async-start(), calls=%async_computation.4 | async-start | bytes 2359296 | tf_op jit(solution)/shard_map/reduce_scatter | solution.py:111
  63.6 262.0 %reduce-scatter.5.cloned.1.call-start = ((), (), s32[]{:S(2)}) async-start(), calls=%async_computation.5 | async-start | bytes 2359296 | tf_op jit(solution)/shard_map/reduce_scatter | solution.py:111
  104.6 3.3 copy-start.11
  104.6 3.3 copy-start.18
  134.7 3.9 %copy-start.2 = (bf16[352,2048]{1,0:T(8,128)(2,1)}, bf16[352,2048]{1,0:T(8,128)(2,1)S(1)}, u32[]{:S(2)}) copy-start(bf16[352,2048]{1,0:T(8,128)(2,1)S(1)} %subtract_convert_fusion.1) | copy-start | bytes 4325380
  135.8 97.8 %copy-start.4 = (bf16[2048,352]{0,1:T(8,128)(2,1)}, bf16[2048,352]{0,1:T(8,128)(2,1)S(1)}, u32[]{:S(2)}) copy-start(bf16[2048,352]{0,1:T(8,128)(2,1)S(1)} %fusion.14) | copy-start | bytes 4325380
  138.6 94.9 %copy-start.6 = (bf16[2048,352]{0,1:T(8,128)(2,1)}, bf16[2048,352]{0,1:T(8,128)(2,1)S(1)}, u32[]{:S(2)}) copy-start(bf16[2048,352]{0,1:T(8,128)(2,1)S(1)} %fusion.15) | copy-start | bytes 4325380
  138.7 34.6 %collective-permute-start.3 = (bf16[2048,352]{0,1:T(8,128)(2,1)S(1)}, bf16[2048,352]{0,1:T(8,128)(2,1)}, u32[]{:S(2)}, u32[]{:S(2)}) collective-permute-start(bf16[2048,352]{0,1:T(8,128)(2,1)S(1)} %get-tuple-element.87), channel_id=1, source_target_pairs={{0,16},{8,24},{16,0},{24,8},{32,48},{40,56},{48,32},{56,40},{64,80... | collective-permute-start | bytes 4325384 | tf_op jit(solution)/shard_map/cond/branch_1_fun/ppermute | solution.py:20
  138.8 65.4 %collective-permute-start.4 = (bf16[2048,352]{0,1:T(8,128)(2,1)S(1)}, bf16[2048,352]{0,1:T(8,128)(2,1)}, u32[]{:S(2)}, u32[]{:S(2)}) collective-permute-start(bf16[2048,352]{0,1:T(8,128)(2,1)S(1)} %get-tuple-element.88), channel_id=1, source_target_pairs={{0,16},{8,24},{16,0},{24,8},{32,48},{40,56},{48,32},{56,40},{64,80... | collective-permute-start | bytes 4325384 | tf_op jit(solution)/shard_map/cond/branch_1_fun/ppermute | solution.py:20
  140.8 89.8 %collective-permute-start.5 = (bf16[352,2048]{1,0:T(8,128)(2,1)S(1)}, bf16[352,2048]{1,0:T(8,128)(2,1)}, u32[]{:S(2)}, u32[]{:S(2)}) collective-permute-start(bf16[352,2048]{1,0:T(8,128)(2,1)S(1)} %get-tuple-element.89), channel_id=1, source_target_pairs={{0,16},{8,24},{16,0},{24,8},{32,48},{40,56},{48,32},{56,40},{64,80... | collective-permute-start | bytes 4325384 | tf_op jit(solution)/shard_map/cond/branch_1_fun/ppermute | solution.py:20
  233.6 4.2 %copy-start.20 = (f32[512,352]{0,1:T(8,128)}, f32[512,352]{0,1:T(8,128)S(1)}, u32[]{:S(2)}) copy-start(f32[512,352]{0,1:T(8,128)S(1)} %convolution_bitcast_fusion) | copy-start | bytes 2162692
  233.6 4.1 %copy-start.3 = (bf16[352,2048]{1,0:T(8,128)(2,1)S(1)}, bf16[352,2048]{1,0:T(8,128)(2,1)}, u32[]{:S(2)}) copy-start(bf16[352,2048]{1,0:T(8,128)(2,1)} %copy-done.2) | copy-start | bytes 4325380
  244.9 4.8 %copy-start.25 = (f32[512,352]{0,1:T(8,128)S(1)}, f32[512,352]{0,1:T(8,128)}, u32[]{:S(2)}) copy-start(f32[512,352]{0,1:T(8,128)} %get-tuple-element.209) | copy-start | bytes 2162692
  283.8 3.6 %copy-start.10 = (f32[352,2048]{1,0:T(8,128)S(1)}, f32[352,2048]{1,0:T(8,128)}, u32[]{:S(2)}) copy-start(f32[352,2048]{1,0:T(8,128)} %get-tuple-element.207) | copy-start | bytes 8650756
  286.4 5.1 %copy-start = (bf16[352,2048]{1,0:T(8,128)(2,1)}, bf16[352,2048]{1,0:T(8,128)(2,1)S(1)}, u32[]{:S(2)}) copy-start(bf16[352,2048]{1,0:T(8,128)(2,1)S(1)} %subtract_convert_fusion) | copy-start | bytes 4325380
  291.6 3.4 %collective-permute-start.12 = (bf16[2048,352]{0,1:T(8,128)(2,1)S(1)}, bf16[2048,352]{0,1:T(8,128)(2,1)}, u32[]{:S(2)}, u32[]{:S(2)}) collective-permute-start(bf16[2048,352]{0,1:T(8,128)(2,1)S(1)} %get-tuple-element.96), channel_id=1, source_target_pairs={{0,8},{8,0},{16,24},{24,16},{32,40},{40,32},{48,56},{56,48},{64,72... | collective-permute-start | bytes 4325384 | tf_op jit(solution)/shard_map/cond/branch_0_fun/ppermute | solution.py:20
  291.7 5.4 %collective-permute-start.13 = (bf16[2048,352]{0,1:T(8,128)(2,1)S(1)}, bf16[2048,352]{0,1:T(8,128)(2,1)}, u32[]{:S(2)}, u32[]{:S(2)}) collective-permute-start(bf16[2048,352]{0,1:T(8,128)(2,1)S(1)} %get-tuple-element.97), channel_id=1, source_target_pairs={{0,8},{8,0},{16,24},{24,16},{32,40},{40,32},{48,56},{56,48},{64,72... | collective-permute-start | bytes 4325384 | tf_op jit(solution)/shard_map/cond/branch_0_fun/ppermute | solution.py:20
  292.2 7.0 %collective-permute-start.14 = (bf16[352,2048]{1,0:T(8,128)(2,1)S(1)}, bf16[352,2048]{1,0:T(8,128)(2,1)}, u32[]{:S(2)}, u32[]{:S(2)}) collective-permute-start(bf16[352,2048]{1,0:T(8,128)(2,1)S(1)} %get-tuple-element.98), channel_id=1, source_target_pairs={{0,8},{8,0},{16,24},{24,16},{32,40},{40,32},{48,56},{56,48},{64,72... | collective-permute-start | bytes 4325384 | tf_op jit(solution)/shard_map/cond/branch_0_fun/ppermute | solution.py:20
  (14 other events, 33.8 us)
Sparse Core Ops, SparseCore 0:
  11.0 87.7 all-gather.4
  101.3 57.1 all-gather.6
  162.5 79.1 reduce-scatter.2
  245.6 80.0 reduce-scatter.4
